TPU v7x, 32 devices: a whole 2x2x4 slice. The times are simulated.
32 devices in a mesh: gx: 4 (over z), gy: 4 (over y, x), gz: 2 (over core).
Axes of the slice: x: 2, y: 2, z: 4, core: 2. Of those that a mesh axis runs over, the one named last changes fastest.
Arguments:
- velocity: float32 [3, 64, 64, 256], P(None, 'gx', 'gy', 'gz'), may hold values from -6 to 6
Outputs:
- stress_residual: float32 [6, 2048], P(None, ('gx', 'gy', 'gz'))
- coefficients: float32 [96, 6], replicated
All inputs are finite; a program needn't handle non-finite values.
Results may differ from a plain program's by a relative error of at most 0.0042.
Values may be sent and summed in bfloat16 or wider, within the bound.
No kernel may reach another device: no remote copies, remote signals or barrier semaphores. Data moves between devices by JAX's collectives and lax.ppermute only.
A program may use at most 64 MiB of HBM per device.

v0:
```python
import jax
import jax.numpy as jnp
import numpy as np
from jax import lax
from jax.sharding import PartitionSpec as P

PRECISE = lax.Precision.HIGHEST
INDEX_PAIRS = ((0, 0), (1, 1), (2, 2), (0, 1), (0, 2), (1, 2))
WIDTHS = (3.0, 6.0, 12.0)


def extended(block, sides, width):
    for axis, dim in sides:
        count = lax.axis_size(axis)
        forward = [(i, i + 1) for i in range(count - 1)]
        forward.append((count - 1, 0))
        backward = [(target, source) for source, target in forward]
        low = lax.ppermute(
            lax.slice_in_dim(block, block.shape[dim] - width, None, axis=dim), axis, forward
        )
        high = lax.ppermute(lax.slice_in_dim(block, 0, width, axis=dim), axis, backward)
        block = jnp.concatenate([low, block, high], axis=dim)
    return block


def window_table(combos):
    weights_table = np.zeros((len(combos), 16), np.float32)
    for row_index in range(len(combos)):
        box_width, offset = combos[row_index]
        low_edge = 7.5 + offset - box_width / 2.0
        high_edge = 7.5 + offset + box_width / 2.0
        for cell_index in range(16):
            cell_share = min(cell_index + 0.5, high_edge) - max(cell_index - 0.5, low_edge)
            weights_table[row_index, cell_index] = max(cell_share, 0.0) / box_width
    return weights_table


def velocity_combos():
    return [(box_width, offset) for box_width in WIDTHS for offset in (-2.0, 0.0, 2.0)]


def product_combos():
    return [(3.0, 0.0), (12.0, 0.0)]


def matrix_product(left_matrix, right_matrix):
    return [
        [
            left_matrix[i][0] * right_matrix[0][j]
            + left_matrix[i][1] * right_matrix[1][j]
            + left_matrix[i][2] * right_matrix[2][j]
            for j in range(3)
        ]
        for i in range(3)
    ]


def pick_pairs(matrix):
    return [matrix[i][j] for i, j in INDEX_PAIRS]


def build_rows(box_means, pair_means):
    feature_rows = []
    centre_values = []
    for width_index in range(3):
        middle = 3 * width_index + 1
        scaled = WIDTHS[width_index] ** 2 * 0.25

        def offset_value(component, direction, step_size):
            position_list = [middle, middle, middle]
            position_list[direction] = middle + step_size
            return box_means[component, position_list[0], position_list[1], position_list[2]]

        centre_values.append([box_means[i, middle, middle, middle] for i in range(3)])
        gradient = [
            [(offset_value(i, j, 1) - offset_value(i, j, -1)) * scaled for j in range(3)]
            for i in range(3)
        ]
        strain = [[(gradient[i][j] + gradient[j][i]) * 0.5 for j in range(3)] for i in range(3)]
        spin_part = [[(gradient[i][j] - gradient[j][i]) * 0.5 for j in range(3)] for i in range(3)]
        square_strain = matrix_product(strain, strain)
        first_order = matrix_product(strain, spin_part)
        second_order = matrix_product(spin_part, strain)
        commutator = [[first_order[i][j] - second_order[i][j] for j in range(3)] for i in range(3)]
        spin_square = matrix_product(spin_part, spin_part)
        magnitude = sum((strain[i][j] * strain[i][j] for i in range(3) for j in range(3)))
        feature_rows += (
            pick_pairs(strain)
            + pick_pairs(square_strain)
            + pick_pairs(commutator)
            + pick_pairs(spin_square)
        )
        feature_rows += [magnitude * entry for entry in pick_pairs(strain)]
    small_box = centre_values[0]
    large_box = centre_values[2]
    feature_rows += [
        pair_means[index, 0] - small_box[i] * small_box[j]
        for index, (i, j) in enumerate(INDEX_PAIRS)
    ]
    target_rows = [
        pair_means[index, 1] - large_box[i] * large_box[j]
        for index, (i, j) in enumerate(INDEX_PAIRS)
    ]
    return (jnp.stack(feature_rows), jnp.stack(target_rows))


def solve_fit(gram_matrix, sample_total):
    scales = jnp.sqrt(jnp.diagonal(gram_matrix) / sample_total + 1e-06)
    feature_scale = scales[:96]
    normal = gram_matrix[:96, :96] / (
        sample_total * feature_scale[:, None] * feature_scale[None, :]
    ) + 0.1 * jnp.eye(96, dtype=jnp.float32)
    target_side = gram_matrix[:96, 96:] / (sample_total * feature_scale[:, None])
    factor = jnp.linalg.cholesky(normal)
    solved = jax.scipy.linalg.cho_solve((factor, True), target_side)
    return (solved / feature_scale[:, None], scales[96:])


def axis_weights(length, weights_table):
    sample_count = length // 8
    combo_count = weights_table.shape[0]
    full_table = np.zeros((sample_count * combo_count, length + 8), np.float32)
    for sample_index in range(sample_count):
        full_table[
            sample_index * combo_count : (sample_index + 1) * combo_count,
            8 * sample_index : 8 * sample_index + 16,
        ] = weights_table
    return jnp.asarray(full_table)


def windowed(wide_field, weights_table):
    along_z = jnp.einsum(
        "cxyz,kz->cxyk",
        wide_field,
        axis_weights(wide_field.shape[3] - 8, weights_table),
        precision=PRECISE,
    )
    along_y = jnp.einsum(
        "cxyk,jy->cxjk",
        along_z,
        axis_weights(wide_field.shape[2] - 8, weights_table),
        precision=PRECISE,
    )
    return jnp.einsum(
        "cxjk,ix->cijk",
        along_y,
        axis_weights(wide_field.shape[1] - 8, weights_table),
        precision=PRECISE,
    )


def shards(velocity):
    rounded = velocity.astype(jnp.bfloat16)
    padded = extended(rounded, (("gx", 1), ("gy", 2), ("gz", 3)), 4)
    wide_field = padded.astype(jnp.float32)
    count_x = velocity.shape[1] // 8
    count_y = velocity.shape[2] // 8
    count_z = velocity.shape[3] // 8
    samples = count_x * count_y * count_z
    box_means = windowed(wide_field, window_table(velocity_combos()))
    box_means = box_means.reshape(3, count_x, 9, count_y, 9, count_z, 9)
    box_means = jnp.transpose(box_means, (0, 2, 4, 6, 1, 3, 5)).reshape(3, 9, 9, 9, samples)
    pair_field = jnp.stack([wide_field[i] * wide_field[j] for i, j in INDEX_PAIRS])
    pair_means = windowed(pair_field, window_table(product_combos())).reshape(
        6, count_x, 2, count_y, 2, count_z, 2
    )
    pair_means = jnp.stack(
        [pair_means[:, :, 0, :, 0, :, 0], pair_means[:, :, 1, :, 1, :, 1]], axis=1
    )
    pair_means = pair_means.reshape(6, 2, samples)
    features, targets = build_rows(box_means, pair_means)
    stacked = jnp.concatenate([features, targets], axis=0)
    local_gram = jnp.dot(stacked, stacked.T, precision=PRECISE, preferred_element_type=jnp.float32)
    gram_matrix = lax.psum(local_gram, ("gx", "gy", "gz"))
    sample_total = float(samples * lax.axis_size("gx") * lax.axis_size("gy") * lax.axis_size("gz"))
    coefficients, target_scale = solve_fit(gram_matrix, sample_total)
    predicted = jnp.dot(
        coefficients.T, features, precision=PRECISE, preferred_element_type=jnp.float32
    )
    residual = (targets - predicted) / target_scale[:, None]
    return (residual, coefficients)


def solution(mesh):
    in_specs = (P(None, "gx", "gy", "gz"),)
    out_specs = (P(None, ("gx", "gy", "gz")), P())
    return jax.shard_map(shards, mesh=mesh, in_specs=in_specs, out_specs=out_specs, check_vma=False)
```

profile of v0, /device:TPU:0, one launch (start us, length us, event | category | flops | bytes accessed | tf_op | source)
XLA Modules:
  0.0 118.4 jit_solution(10109509089073360371)
XLA Ops:
  0.6 1.0 convert_element_type.7
  1.7 3.1 %collective-permute-start = (bf16[3,4,16,128]{3,2,1,0:T(8,128)(2,1)S(1)}, bf16[3,4,16,128]{3,2,1,0:T(8,128)(2,1)S(1)}, u32[]{:S(2)}, u32[]{:S(2)}) collective-permute-start(bf16[3,4,16,128]{3,2,1,0:T(8,128)(2,1)S(1)} %get-tuple-element.102), channel_id=1, source_target_pairs={{0,8},{8,16},{16,24},{24,0},{1,9},{9,17},{17,25},{25,1},{2,10},{10... | collective-permute-start | bytes 147464 | tf_op jit(solution)/shard_map/ppermute | solution.py:18
  4.8 2.1 %collective-permute-start.1 = (bf16[3,4,16,128]{3,2,1,0:T(8,128)(2,1)S(1)}, bf16[3,4,16,128]{3,2,1,0:T(8,128)(2,1)S(1)}, u32[]{:S(2)}, u32[]{:S(2)}) collective-permute-start(bf16[3,4,16,128]{3,2,1,0:T(8,128)(2,1)S(1)} %get-tuple-element.103), channel_id=1, source_target_pairs={{8,0},{16,8},{24,16},{0,24},{9,1},{17,9},{25,17},{1,25},{10,2},{18... | collective-permute-start | bytes 147464 | tf_op jit(solution)/shard_map/ppermute | solution.py:21
  6.9 2.1 %collective-permute-done = bf16[3,4,16,128]{3,2,1,0:T(8,128)(2,1)S(1)} collective-permute-done((bf16[3,4,16,128]{3,2,1,0:T(8,128)(2,1)S(1)}, bf16[3,4,16,128]{3,2,1,0:T(8,128)(2,1)S(1)}, u32[]{:S(2)}, u32[]{:S(2)}) %collective-permute-start) | collective-permute-done | bytes 49184 | tf_op jit(solution)/shard_map/ppermute | solution.py:18
  9.5 1.5 %collective-permute-start.2 = (bf16[3,24,4,128]{3,2,1,0:T(4,128)(2,1)S(1)}, bf16[3,24,4,128]{3,2,1,0:T(4,128)(2,1)S(1)}, u32[]{:S(2)}, u32[]{:S(2)}) collective-permute-start(bf16[3,24,4,128]{3,2,1,0:T(4,128)(2,1)S(1)} %get-tuple-element.100), channel_id=1, source_target_pairs={{0,2},{2,4},{4,6},{6,0},{1,3},{3,5},{5,7},{7,1},{8,10},{10,12},{12... | collective-permute-start | bytes 221192 | tf_op jit(solution)/shard_map/ppermute | solution.py:18
  11.0 1.4 %collective-permute-start.3 = (bf16[3,24,4,128]{3,2,1,0:T(4,128)(2,1)S(1)}, bf16[3,24,4,128]{3,2,1,0:T(4,128)(2,1)S(1)}, u32[]{:S(2)}, u32[]{:S(2)}) collective-permute-start(bf16[3,24,4,128]{3,2,1,0:T(4,128)(2,1)S(1)} %get-tuple-element.101), channel_id=1, source_target_pairs={{2,0},{4,2},{6,4},{0,6},{3,1},{5,3},{7,5},{1,7},{10,8},{12,10},{14... | collective-permute-start | bytes 221192 | tf_op jit(solution)/shard_map/ppermute | solution.py:21
  12.5 2.3 %collective-permute-done.2 = bf16[3,24,4,128]{3,2,1,0:T(4,128)(2,1)S(1)} collective-permute-done((bf16[3,24,4,128]{3,2,1,0:T(4,128)(2,1)S(1)}, bf16[3,24,4,128]{3,2,1,0:T(4,128)(2,1)S(1)}, u32[]{:S(2)}, u32[]{:S(2)}) %collective-permute-start.2) | collective-permute-done | bytes 73760 | tf_op jit(solution)/shard_map/ppermute | solution.py:18
  14.8 0.8 collective-permute-done.3
  16.7 1.3 %collective-permute-done.4 = bf16[3,24,24,4]{3,2,1,0:T(8,128)(2,1)S(1)} collective-permute-done((bf16[3,24,24,4]{3,2,1,0:T(8,128)(2,1)S(1)}, bf16[3,24,24,4]{3,2,1,0:T(8,128)(2,1)S(1)}, u32[]{:S(2)}, u32[]{:S(2)}) %collective-permute-start.4) | collective-permute-done | bytes 13856 | tf_op jit(solution)/shard_map/ppermute | solution.py:18
  18.6 1.3 %fusion.124 = f32[3,24,24,144]{3,2,1,0:T(8,128)S(1)} fusion(f32[144,136,1,1]{0,1,3,2:T(8,128)S(1)} %copy-done.8, bf16[3,24,24,4]{3,2,1,0:T(8,128)(2,1)S(1)} %collective-permute-done.5, bf16[3,24,4,128]{3,2,1,0:T(4,128)(2,1)S(1)} %collective-permute-done.3, bf16[3,4,16,128]{3,2,1,0:T(8,128)(2,1)S(1)} %collective-permute-done.1, ...), kind=kOutput, calls=%fused_computation.402 | convolution fusion | flops 409383936 | bytes 1543680 | tf_op jit(solution)/shard_map/cxyz,kz->cxyk/dot_general | solution.py:132
  19.9 1.6 %convolution_bitcast_fusion = f32[3,24,18,144]{3,2,1,0:T(8,128)S(1)} fusion(f32[3,24,24,144]{3,2,1,0:T(8,128)S(1)} %fusion.124, f32[18,24,1,1]{1,0,3,2:T(8,128)S(1)} %copy-done.4), kind=kOutput, calls=%fused_computation.1 | convolution fusion | flops 53747712 | bytes 1743552 | tf_op jit(solution)/shard_map/cxyk,jy->cxjk/dot_general | solution.py:138
  21.5 1.6 %convolution_bitcast_fusion.1 = f32[3,18,18,144]{3,1,2,0:T(8,128)S(1)} fusion(f32[18,24,1,1]{1,0,3,2:T(8,128)S(1)} %copy-done.4, f32[3,24,18,144]{3,2,1,0:T(8,128)S(1)} %convolution_bitcast_fusion), kind=kOutput, calls=%fused_computation.2 | convolution fusion | flops 40310784 | bytes 1308096 | tf_op jit(solution)/shard_map/cxjk,ix->cijk/dot_general | solution.py:144
  23.5 6.3 %reshape.6592 = f32[3,2,9,2,9,16,9]{6,5,4,3,2,1,0:T(8,128)} reshape(f32[3,18,18,144]{3,2,1,0:T(8,128)S(1)} %copy.30) | data formatting | bytes 1119744 | tf_op jit(solution)/shard_map/reshape | solution.py:161
  29.8 11.0 %copy.31 = f32[3,9,9,9,2,2,16]{6,5,4,0,3,2,1:T(2,128)} copy(f32[3,9,9,9,2,2,16]{3,6,2,5,1,4,0:T(8,128)} %bitcast.897) | data formatting | bytes 1119744 | tf_op jit(solution)/shard_map/transpose | solution.py:162
  40.8 5.8 %reshape.6593 = f32[3,9,9,9,64]{4,0,3,2,1:T(4,128)S(1)} reshape(f32[3,9,9,9,2,2,16]{6,5,4,0,3,2,1:T(2,128)} %copy.31) | data formatting | bytes 1119744 | tf_op jit(solution)/shard_map/reshape | solution.py:162
  46.7 0.8 fusion.125
  48.5 2.9 %fusion.158 = f32[6,24,24,32]{3,2,1,0:T(8,128)S(1)} fusion(f32[6,24,24,136]{3,2,1,0:T(8,128)S(1)} %multiply_dynamic-update-slice_fusion, f32[32,136,1,1]{1,0,3,2:T(8,128)S(1)} %copy-done.5), kind=kOutput, calls=%fused_computation.409 | convolution fusion | flops 180486144 | bytes 2339840 | tf_op jit(solution)/shard_map/cxyz,kz->cxyk/dot_general | solution.py:132
  51.4 1.0 convolution_bitcast_fusion.2
  52.9 2.0 %slice_reduce_fusion = (f32[2,2,16]{2,1,0:T(2,128)S(1)}, f32[2,2,16]{2,1,0:T(2,128)S(1)}, f32[2,2,16]{2,1,0:T(2,128)S(1)}, f32[2,2,16]{2,1,0:T(2,128)S(1)}, f32[...) fusion(f32[6,2,2,2,2,16,2]{0,6,5,4,3,2,1:T(2,128)S(1)} %bitcast.898), kind=kLoop, calls=%fused_computation.34 | loop fusion | bytes 6144 | tf_op jit(solution)/shard_map/slice | solution.py:97
  57.3 40.3 %psum.7 = f32[102,102]{1,0:T(8,128)S(1)} all-reduce(f32[102,102]{1,0:T(8,128)S(1)} %fusion.159), channel_id=1, replica_groups=mesh['gx'=4,'gy'=4,'gz'=2] {'gx','gy','gz'}, use_global_device_ids=true, to_apply=%region_0.0 | all-reduce | flops 10404 | bytes 83232 | tf_op jit(solution)/shard_map/psum | solution.py:174
  97.6 1.7 %gather_fusion = f32[102]{0:T(128)S(1)} fusion(f32[102,102]{1,0:T(8,128)S(1)} %psum.7, s32[102]{0:T(128)S(1)} %or_bitcast_fusion), kind=kCustom, calls=%fused_computation | custom fusion | bytes 1632 | tf_op jit(solution)/shard_map/jit(diagonal)/cond/branch_0_fun/gather | solution.py:108
  99.6 8.8 %cholesky.16 = f32[96,96]{1,0:T(8,128)S(1)} custom-call(f32[96,96]{1,0:T(8,128)S(1)} %fusion.8), custom_call_target="Cholesky" | custom-call | tf_op jit(solution)/shard_map/jit(cholesky)/cholesky | solution.py:114
  109.7 7.4 %custom-call.10 = f32[1,96,96]{1,2,0:T(8,128)S(1)} custom-call(f32[1,96,96]{2,1,0:T(8,128)S(1)} %fusion.3), custom_call_target="InvertDiagBlocksLowerTriangular" | custom-call | tf_op jit(solution)/shard_map/jit(_cho_solve)/triangular_solve | solution.py:115
  117.6 0.8 fusion.1
  (86 shorter events, 8.3 us)
Async XLA Ops:
  1.7 16.9 %copy-start.8 = (f32[144,136,1,1]{0,1,3,2:T(8,128)S(1)}, f32[144,136,1,1]{0,1,3,2:T(8,128)}, u32[]{:S(2)}) copy-start(f32[144,136,1,1]{0,1,3,2:T(8,128)} %constant.98) | copy-start | bytes 235012
  1.7 7.3 %collective-permute-start = (bf16[3,4,16,128]{3,2,1,0:T(8,128)(2,1)S(1)}, bf16[3,4,16,128]{3,2,1,0:T(8,128)(2,1)S(1)}, u32[]{:S(2)}, u32[]{:S(2)}) collective-permute-start(bf16[3,4,16,128]{3,2,1,0:T(8,128)(2,1)S(1)} %get-tuple-element.102), channel_id=1, source_target_pairs={{0,8},{8,16},{16,24},{24,0},{1,9},{9,17},{17,25},{25,1},{2,10},{10... | collective-permute-start | bytes 147464 | tf_op jit(solution)/shard_map/ppermute | solution.py:18
  4.8 4.6 %collective-permute-start.1 = (bf16[3,4,16,128]{3,2,1,0:T(8,128)(2,1)S(1)}, bf16[3,4,16,128]{3,2,1,0:T(8,128)(2,1)S(1)}, u32[]{:S(2)}, u32[]{:S(2)}) collective-permute-start(bf16[3,4,16,128]{3,2,1,0:T(8,128)(2,1)S(1)} %get-tuple-element.103), channel_id=1, source_target_pairs={{8,0},{16,8},{24,16},{0,24},{9,1},{17,9},{25,17},{1,25},{10,2},{18... | collective-permute-start | bytes 147464 | tf_op jit(solution)/shard_map/ppermute | solution.py:21
  9.4 10.5 %copy-start.2 = (bf16[3,4,16,128]{3,2,1,0:T(8,128)(2,1)}, bf16[3,4,16,128]{3,2,1,0:T(8,128)(2,1)S(1)}, u32[]{:S(2)}) copy-start(bf16[3,4,16,128]{3,2,1,0:T(8,128)(2,1)S(1)} %collective-permute-done.1) | copy-start | bytes 147460
  9.5 5.3 %collective-permute-start.2 = (bf16[3,24,4,128]{3,2,1,0:T(4,128)(2,1)S(1)}, bf16[3,24,4,128]{3,2,1,0:T(4,128)(2,1)S(1)}, u32[]{:S(2)}, u32[]{:S(2)}) collective-permute-start(bf16[3,24,4,128]{3,2,1,0:T(4,128)(2,1)S(1)} %get-tuple-element.100), channel_id=1, source_target_pairs={{0,2},{2,4},{4,6},{6,0},{1,3},{3,5},{5,7},{7,1},{8,10},{10,12},{12... | collective-permute-start | bytes 221192 | tf_op jit(solution)/shard_map/ppermute | solution.py:18
  11.0 4.6 %collective-permute-start.3 = (bf16[3,24,4,128]{3,2,1,0:T(4,128)(2,1)S(1)}, bf16[3,24,4,128]{3,2,1,0:T(4,128)(2,1)S(1)}, u32[]{:S(2)}, u32[]{:S(2)}) collective-permute-start(bf16[3,24,4,128]{3,2,1,0:T(4,128)(2,1)S(1)} %get-tuple-element.101), channel_id=1, source_target_pairs={{2,0},{4,2},{6,4},{0,6},{3,1},{5,3},{7,5},{1,7},{10,8},{12,10},{14... | collective-permute-start | bytes 221192 | tf_op jit(solution)/shard_map/ppermute | solution.py:21
  16.1 1.9 %collective-permute-start.4 = (bf16[3,24,24,4]{3,2,1,0:T(8,128)(2,1)S(1)}, bf16[3,24,24,4]{3,2,1,0:T(8,128)(2,1)S(1)}, u32[]{:S(2)}, u32[]{:S(2)}) collective-permute-start(bf16[3,24,24,4]{3,2,1,0:T(8,128)(2,1)S(1)} %get-tuple-element.98), channel_id=1, source_target_pairs={{0,1},{1,0},{2,3},{3,2},{4,5},{5,4},{6,7},{7,6},{8,9},{9,8},{10,11... | collective-permute-start | bytes 41480 | tf_op jit(solution)/shard_map/ppermute | solution.py:18
  16.2 2.4 %collective-permute-start.5 = (bf16[3,24,24,4]{3,2,1,0:T(8,128)(2,1)S(1)}, bf16[3,24,24,4]{3,2,1,0:T(8,128)(2,1)S(1)}, u32[]{:S(2)}, u32[]{:S(2)}) collective-permute-start(bf16[3,24,24,4]{3,2,1,0:T(8,128)(2,1)S(1)} %get-tuple-element.99), channel_id=1, source_target_pairs={{1,0},{0,1},{3,2},{2,3},{5,4},{4,5},{7,6},{6,7},{9,8},{8,9},{11,10... | collective-permute-start | bytes 41480 | tf_op jit(solution)/shard_map/ppermute | solution.py:21
  16.7 3.3 %copy-start.4 = (f32[18,24,1,1]{1,0,3,2:T(8,128)S(1)}, f32[18,24,1,1]{1,0,3,2:T(8,128)}, u32[]{:S(2)}) copy-start(f32[18,24,1,1]{1,0,3,2:T(8,128)} %constant.99) | copy-start | bytes 5188
  18.6 1.3 %copy-start = (bf16[3,24,24,4]{3,2,1,0:T(8,128)(2,1)}, bf16[3,24,24,4]{3,2,1,0:T(8,128)(2,1)S(1)}, u32[]{:S(2)}) copy-start(bf16[3,24,24,4]{3,2,1,0:T(8,128)(2,1)S(1)} %collective-permute-done.5) | copy-start | bytes 41476
  40.8 5.9 %copy-start.1 = (bf16[3,24,24,4]{3,2,1,0:T(8,128)(2,1)S(1)}, bf16[3,24,24,4]{3,2,1,0:T(8,128)(2,1)}, u32[]{:S(2)}) copy-start(bf16[3,24,24,4]{3,2,1,0:T(8,128)(2,1)} %copy-done) | copy-start | bytes 41476
  40.8 5.9 %copy-start.3 = (bf16[3,4,16,128]{3,2,1,0:T(8,128)(2,1)S(1)}, bf16[3,4,16,128]{3,2,1,0:T(8,128)(2,1)}, u32[]{:S(2)}) copy-start(bf16[3,4,16,128]{3,2,1,0:T(8,128)(2,1)} %copy-done.2) | copy-start | bytes 147460
  47.7 0.8 copy-start.5
  48.5 2.9 %copy-start.6 = (f32[4,24,1,1]{1,0,3,2:T(4,128)S(1)}, f32[4,24,1,1]{1,0,3,2:T(4,128)}, u32[]{:S(2)}) copy-start(f32[4,24,1,1]{1,0,3,2:T(4,128)} %constant.97) | copy-start | bytes 1156
  117.6 0.8 copy-start.7
where the time goes:
time: 119 us; the launch traced here: 118 us
  blocking collectives  40.3 us (34%)
  local copies, waits for them, and re-layouts  29.8 us (25%)
  other arithmetic  20.6 us (17%)
  matrix products  10.3 us (9%)
  starting transfers between devices  8.74 us (7%)
  waiting for transfers between devices  7.6 us (6%)
    psum x1, blocking collectives, shards(): gram_matrix = lax.psum(local_gram, ('gx', 'gy', 'gz'))  40.3 us
    transpose x1, local copies, waits for them, and re-layouts, shards(): jnp.transpose(box_means, (0, 2, 4, 6, 1, 3, 5)).reshape(3, 9, 9, 9, samples)  11 us
    another operation x3, other arithmetic, solve_fit(): factor = jnp.linalg.cholesky(normal)  9.45 us
    another operation x2, other arithmetic, solve_fit(): solved = jax.scipy.linalg.cho_solve((factor, True), target_side)  8.01 us
    reshape x1, local copies, waits for them, and re-layouts, shards(): box_means = box_means.reshape(3, count_x, 9, count_y, 9, count_z, 9)  6.35 us
    reshape x1, local copies, waits for them, and re-layouts, shards(): jnp.transpose(box_means, (0, 2, 4, 6, 1, 3, 5)).reshape(3, 9, 9, 9, samples)  5.76 us
    ppermute x3, waiting for transfers between devices, extended(): lax.ppermute(lax.slice_in_dim(block, block.shape[dim] - width, None, axis...  5.7 us
    ppermute x3, starting transfers between devices, extended(): lax.ppermute(lax.slice_in_dim(block, block.shape[dim] - width, None, axis...  4.72 us
  transfers between devices with their start and end apart: 6, of which 6 were waited for; matrix products, arithmetic and copies ran while one was open for 0% of the time, Pallas kernels for 0%

commit v1 on v0

--- a/solution.py
+++ b/solution.py
@@ -171,7 +171,7 @@
     features, targets = build_rows(box_means, pair_means)
     stacked = jnp.concatenate([features, targets], axis=0)
     local_gram = jnp.dot(stacked, stacked.T, precision=PRECISE, preferred_element_type=jnp.float32)
-    gram_matrix = lax.psum(local_gram, ("gx", "gy", "gz"))
+    gram_matrix = jnp.sum(lax.all_gather(local_gram, ("gx", "gy", "gz")), axis=0)
     sample_total = float(samples * lax.axis_size("gx") * lax.axis_size("gy") * lax.axis_size("gz"))
     coefficients, target_scale = solve_fit(gram_matrix, sample_total)
     predicted = jnp.dot(

time: 119 us -> 150 us (1.26)
  waiting for transfers between devices: 7.6 us -> 63.5 us
  blocking collectives: 40.3 us -> 0 us
  between operations: 1.07 us -> 14.4 us
  other arithmetic: 20.6 us -> 22.2 us
    all_gather x0 -> x1, waiting for transfers between devices: none -> 55.9 us  [shards(): lax.all_gather(local_gram, ('gx', 'gy', 'gz'))]
    psum x1 -> x0, blocking collectives: 40.3 us -> none  [shards(): gram_matrix = lax.psum(local_gram, ('gx', 'gy', 'gz'))]
    reduce_sum x0 -> x1, other arithmetic: none -> 1.59 us  [shards(): jnp.sum(lax.all_gather(local_gram, ('gx', 'gy', 'gz')), axis=0)]
  transfers between devices with their start and end apart: 6 -> 7, of which waited for: 6 -> 7; matrix products, arithmetic and copies ran while one was open for 0% -> 0% of each run, Pallas kernels for 0% -> 0%
where the time goes in v1:
time: 150 us
  waiting for transfers between devices  63.5 us (42%)
  local copies, waits for them, and re-layouts  30 us (20%)
  other arithmetic  22.2 us (15%)
  between operations  14.4 us (10%)
  matrix products  10.9 us (7%)
  starting transfers between devices  8.77 us (6%)
    all_gather x1, waiting for transfers between devices, shards(): lax.all_gather(local_gram, ('gx', 'gy', 'gz'))  55.9 us
    transpose x1, local copies, waits for them, and re-layouts, shards(): jnp.transpose(box_means, (0, 2, 4, 6, 1, 3, 5)).reshape(3, 9, 9, 9, samples)  10.9 us
    another operation x3, other arithmetic, solve_fit(): factor = jnp.linalg.cholesky(normal)  9.45 us
    another operation x2, other arithmetic, solve_fit(): solved = jax.scipy.linalg.cho_solve((factor, True), target_side)  8.01 us
    reshape x1, local copies, waits for them, and re-layouts, shards(): box_means = box_means.reshape(3, count_x, 9, count_y, 9, count_z, 9)  6.35 us
    ppermute x3, waiting for transfers between devices, extended(): lax.ppermute(lax.slice_in_dim(block, block.shape[dim] - width, None, axis...  5.71 us
    reshape x1, local copies, waits for them, and re-layouts, shards(): jnp.transpose(box_means, (0, 2, 4, 6, 1, 3, 5)).reshape(3, 9, 9, 9, samples)  5.7 us
    ppermute x3, starting transfers between devices, extended(): lax.ppermute(lax.slice_in_dim(block, block.shape[dim] - width, None, axis...  4.72 us
  transfers between devices with their start and end apart: 7, of which 7 were waited for; matrix products, arithmetic and copies ran while one was open for 0% of the time, Pallas kernels for 0%

profile of v1, /device:TPU:0, one launch (start us, length us, event | category | flops | bytes accessed | tf_op | source)
XLA Modules:
  0.0 149.7 jit_solution(12968100625260086564)
XLA Ops:
  7.2 1.0 convert_element_type.7
  8.3 3.1 %collective-permute-start = (bf16[3,4,16,128]{3,2,1,0:T(8,128)(2,1)S(1)}, bf16[3,4,16,128]{3,2,1,0:T(8,128)(2,1)S(1)}, u32[]{:S(2)}, u32[]{:S(2)}) collective-permute-start(bf16[3,4,16,128]{3,2,1,0:T(8,128)(2,1)S(1)} %get-tuple-element.102), channel_id=1, source_target_pairs={{0,8},{8,16},{16,24},{24,0},{1,9},{9,17},{17,25},{25,1},{2,10},{10... | collective-permute-start | bytes 147464 | tf_op jit(solution)/shard_map/ppermute | solution.py:18
  11.4 2.1 %collective-permute-start.1 = (bf16[3,4,16,128]{3,2,1,0:T(8,128)(2,1)S(1)}, bf16[3,4,16,128]{3,2,1,0:T(8,128)(2,1)S(1)}, u32[]{:S(2)}, u32[]{:S(2)}) collective-permute-start(bf16[3,4,16,128]{3,2,1,0:T(8,128)(2,1)S(1)} %get-tuple-element.103), channel_id=1, source_target_pairs={{8,0},{16,8},{24,16},{0,24},{9,1},{17,9},{25,17},{1,25},{10,2},{18... | collective-permute-start | bytes 147464 | tf_op jit(solution)/shard_map/ppermute | solution.py:21
  13.5 2.1 %collective-permute-done = bf16[3,4,16,128]{3,2,1,0:T(8,128)(2,1)S(1)} collective-permute-done((bf16[3,4,16,128]{3,2,1,0:T(8,128)(2,1)S(1)}, bf16[3,4,16,128]{3,2,1,0:T(8,128)(2,1)S(1)}, u32[]{:S(2)}, u32[]{:S(2)}) %collective-permute-start) | collective-permute-done | bytes 49184 | tf_op jit(solution)/shard_map/ppermute | solution.py:18
  16.1 1.5 %collective-permute-start.2 = (bf16[3,24,4,128]{3,2,1,0:T(4,128)(2,1)S(1)}, bf16[3,24,4,128]{3,2,1,0:T(4,128)(2,1)S(1)}, u32[]{:S(2)}, u32[]{:S(2)}) collective-permute-start(bf16[3,24,4,128]{3,2,1,0:T(4,128)(2,1)S(1)} %get-tuple-element.100), channel_id=1, source_target_pairs={{0,2},{2,4},{4,6},{6,0},{1,3},{3,5},{5,7},{7,1},{8,10},{10,12},{12... | collective-permute-start | bytes 221192 | tf_op jit(solution)/shard_map/ppermute | solution.py:18
  17.6 1.4 collective-permute-start.3
  19.0 2.3 %collective-permute-done.2 = bf16[3,24,4,128]{3,2,1,0:T(4,128)(2,1)S(1)} collective-permute-done((bf16[3,24,4,128]{3,2,1,0:T(4,128)(2,1)S(1)}, bf16[3,24,4,128]{3,2,1,0:T(4,128)(2,1)S(1)}, u32[]{:S(2)}, u32[]{:S(2)}) %collective-permute-start.2) | collective-permute-done | bytes 73760 | tf_op jit(solution)/shard_map/ppermute | solution.py:18
  21.4 0.8 collective-permute-done.3
  23.2 1.3 collective-permute-done.4
  25.1 1.3 fusion.124
  26.5 1.6 %convolution_bitcast_fusion = f32[3,24,18,144]{3,2,1,0:T(8,128)S(1)} fusion(f32[3,24,24,144]{3,2,1,0:T(8,128)S(1)} %fusion.124, f32[18,24,1,1]{1,0,3,2:T(8,128)S(1)} %copy-done), kind=kOutput, calls=%fused_computation.1 | convolution fusion | flops 53747712 | bytes 1743552 | tf_op jit(solution)/shard_map/cxyk,jy->cxjk/dot_general | solution.py:138
  28.1 1.6 %convolution_bitcast_fusion.1 = f32[3,18,18,144]{3,1,2,0:T(8,128)S(1)} fusion(f32[18,24,1,1]{1,0,3,2:T(8,128)S(1)} %copy-done, f32[3,24,18,144]{3,2,1,0:T(8,128)S(1)} %convolution_bitcast_fusion), kind=kOutput, calls=%fused_computation.2 | convolution fusion | flops 40310784 | bytes 1308096 | tf_op jit(solution)/shard_map/cxjk,ix->cijk/dot_general | solution.py:144
  30.0 6.3 %reshape.6592 = f32[3,2,9,2,9,16,9]{6,5,4,3,2,1,0:T(8,128)} reshape(f32[3,18,18,144]{3,2,1,0:T(8,128)S(1)} %copy.36) | data formatting | bytes 1119744 | tf_op jit(solution)/shard_map/reshape | solution.py:161
  36.4 10.9 %copy.37 = f32[3,9,9,9,2,2,16]{6,5,4,0,3,2,1:T(2,128)} copy(f32[3,9,9,9,2,2,16]{3,6,2,5,1,4,0:T(8,128)} %bitcast.899) | data formatting | bytes 1119744 | tf_op jit(solution)/shard_map/transpose | solution.py:162
  47.3 5.7 %reshape.6593 = f32[3,9,9,9,64]{4,0,3,2,1:T(4,128)S(1)} reshape(f32[3,9,9,9,2,2,16]{6,5,4,0,3,2,1:T(2,128)} %copy.37) | data formatting | bytes 1119744 | tf_op jit(solution)/shard_map/reshape | solution.py:162
  54.9 2.9 %fusion.158 = f32[6,24,24,32]{3,2,1,0:T(8,128)S(1)} fusion(f32[6,24,24,136]{3,2,1,0:T(8,128)S(1)} %multiply_dynamic-update-slice_fusion, f32[32,136,1,1]{1,0,3,2:T(8,128)S(1)} %copy-done.1), kind=kOutput, calls=%fused_computation.410 | convolution fusion | flops 180486144 | bytes 2339840 | tf_op jit(solution)/shard_map/cxyz,kz->cxyk/dot_general | solution.py:132
  57.9 1.0 convolution_bitcast_fusion.2
  59.4 2.0 %slice_reduce_fusion = (f32[2,2,16]{2,1,0:T(2,128)S(1)}, f32[2,2,16]{2,1,0:T(2,128)S(1)}, f32[2,2,16]{2,1,0:T(2,128)S(1)}, f32[2,2,16]{2,1,0:T(2,128)S(1)}, f32[...) fusion(f32[6,2,2,2,2,16,2]{0,6,5,4,3,2,1:T(2,128)S(1)} %bitcast.900), kind=kLoop, calls=%fused_computation.35 | loop fusion | bytes 6144 | tf_op jit(solution)/shard_map/slice | solution.py:97
  63.2 0.9 convolution_bitcast_fusion.3
  64.4 55.9 %all-gather.4.cloned.1.call-done = f32[32,102,102]{2,1,0:T(8,128)} async-done(((f32[1,102,102]{2,1,0:T(8,128)}), f32[32,102,102]{2,1,0:T(8,128)}) %all-gather.4.cloned.1.call-update) | async-done | bytes 1331728 | tf_op jit(solution)/shard_map/all_gather | solution.py:174
  120.2 1.6 %reduce_sum.9 = f32[102,102]{1,0:T(8,128)S(1)} reduce(f32[32,102,102]{2,1,0:T(8,128)} %all-gather.4.cloned.1.call-done, f32[]{:T(128)} %constant.73.clone.1), dimensions={0}, to_apply=%region_0.0 | reduce | flops 322524 | bytes 1373332 | tf_op jit(solution)/shard_map/reduce_sum | solution.py:174
  121.8 1.9 %gather_fusion = f32[102]{0:T(128)S(1)} fusion(f32[102,102]{1,0:T(8,128)S(1)} %reduce_sum.9, s32[102]{0:T(128)S(1)} %or_bitcast_fusion), kind=kCustom, calls=%fused_computation | custom fusion | bytes 1632 | tf_op jit(solution)/shard_map/jit(diagonal)/cond/branch_0_fun/gather | solution.py:108
  124.1 8.8 %cholesky.16 = f32[96,96]{1,0:T(8,128)S(1)} custom-call(f32[96,96]{1,0:T(8,128)S(1)} %fusion.8), custom_call_target="Cholesky" | custom-call | tf_op jit(solution)/shard_map/jit(cholesky)/cholesky | solution.py:114
  134.2 7.4 %custom-call.10 = f32[1,96,96]{1,2,0:T(8,128)S(1)} custom-call(f32[1,96,96]{2,1,0:T(8,128)S(1)} %fusion.3), custom_call_target="InvertDiagBlocksLowerTriangular" | custom-call | tf_op jit(solution)/shard_map/jit(_cho_solve)/triangular_solve | solution.py:115
  (81 shorter events, 9.7 us)
Async XLA Ops:
  7.2 113.1 %all-gather.4.cloned.1.call-start = ((), (), s32[]{:S(2)}) async-start(), calls=%async_computation | async-start | bytes 1757184 | tf_op jit(solution)/shard_map/all_gather | solution.py:174
  8.2 16.9 %copy-start.4 = (f32[144,136,1,1]{0,1,3,2:T(8,128)S(1)}, f32[144,136,1,1]{0,1,3,2:T(8,128)}, u32[]{:S(2)}) copy-start(f32[144,136,1,1]{0,1,3,2:T(8,128)} %constant.99) | copy-start | bytes 235012
  8.3 7.3 %collective-permute-start = (bf16[3,4,16,128]{3,2,1,0:T(8,128)(2,1)S(1)}, bf16[3,4,16,128]{3,2,1,0:T(8,128)(2,1)S(1)}, u32[]{:S(2)}, u32[]{:S(2)}) collective-permute-start(bf16[3,4,16,128]{3,2,1,0:T(8,128)(2,1)S(1)} %get-tuple-element.102), channel_id=1, source_target_pairs={{0,8},{8,16},{16,24},{24,0},{1,9},{9,17},{17,25},{25,1},{2,10},{10... | collective-permute-start | bytes 147464 | tf_op jit(solution)/shard_map/ppermute | solution.py:18
  11.4 4.6 %collective-permute-start.1 = (bf16[3,4,16,128]{3,2,1,0:T(8,128)(2,1)S(1)}, bf16[3,4,16,128]{3,2,1,0:T(8,128)(2,1)S(1)}, u32[]{:S(2)}, u32[]{:S(2)}) collective-permute-start(bf16[3,4,16,128]{3,2,1,0:T(8,128)(2,1)S(1)} %get-tuple-element.103), channel_id=1, source_target_pairs={{8,0},{16,8},{24,16},{0,24},{9,1},{17,9},{25,17},{1,25},{10,2},{18... | collective-permute-start | bytes 147464 | tf_op jit(solution)/shard_map/ppermute | solution.py:21
  16.1 5.3 %collective-permute-start.2 = (bf16[3,24,4,128]{3,2,1,0:T(4,128)(2,1)S(1)}, bf16[3,24,4,128]{3,2,1,0:T(4,128)(2,1)S(1)}, u32[]{:S(2)}, u32[]{:S(2)}) collective-permute-start(bf16[3,24,4,128]{3,2,1,0:T(4,128)(2,1)S(1)} %get-tuple-element.100), channel_id=1, source_target_pairs={{0,2},{2,4},{4,6},{6,0},{1,3},{3,5},{5,7},{7,1},{8,10},{10,12},{12... | collective-permute-start | bytes 221192 | tf_op jit(solution)/shard_map/ppermute | solution.py:18
  17.6 4.6 %collective-permute-start.3 = (bf16[3,24,4,128]{3,2,1,0:T(4,128)(2,1)S(1)}, bf16[3,24,4,128]{3,2,1,0:T(4,128)(2,1)S(1)}, u32[]{:S(2)}, u32[]{:S(2)}) collective-permute-start(bf16[3,24,4,128]{3,2,1,0:T(4,128)(2,1)S(1)} %get-tuple-element.101), channel_id=1, source_target_pairs={{2,0},{4,2},{6,4},{0,6},{3,1},{5,3},{7,5},{1,7},{10,8},{12,10},{14... | collective-permute-start | bytes 221192 | tf_op jit(solution)/shard_map/ppermute | solution.py:21
  22.7 1.9 %collective-permute-start.4 = (bf16[3,24,24,4]{3,2,1,0:T(8,128)(2,1)S(1)}, bf16[3,24,24,4]{3,2,1,0:T(8,128)(2,1)S(1)}, u32[]{:S(2)}, u32[]{:S(2)}) collective-permute-start(bf16[3,24,24,4]{3,2,1,0:T(8,128)(2,1)S(1)} %get-tuple-element.98), channel_id=1, source_target_pairs={{0,1},{1,0},{2,3},{3,2},{4,5},{5,4},{6,7},{7,6},{8,9},{9,8},{10,11... | collective-permute-start | bytes 41480 | tf_op jit(solution)/shard_map/ppermute | solution.py:18
  22.7 3.7 %copy-start = (f32[18,24,1,1]{1,0,3,2:T(8,128)S(1)}, f32[18,24,1,1]{1,0,3,2:T(8,128)}, u32[]{:S(2)}) copy-start(f32[18,24,1,1]{1,0,3,2:T(8,128)} %constant.100) | copy-start | bytes 5188
  22.7 2.4 %collective-permute-start.5 = (bf16[3,24,24,4]{3,2,1,0:T(8,128)(2,1)S(1)}, bf16[3,24,24,4]{3,2,1,0:T(8,128)(2,1)S(1)}, u32[]{:S(2)}, u32[]{:S(2)}) collective-permute-start(bf16[3,24,24,4]{3,2,1,0:T(8,128)(2,1)S(1)} %get-tuple-element.99), channel_id=1, source_target_pairs={{1,0},{0,1},{3,2},{2,3},{5,4},{4,5},{7,6},{6,7},{9,8},{8,9},{11,10... | collective-permute-start | bytes 41480 | tf_op jit(solution)/shard_map/ppermute | solution.py:21
  54.2 0.8 copy-start.1
  54.9 2.9 %copy-start.2 = (f32[4,24,1,1]{1,0,3,2:T(4,128)S(1)}, f32[4,24,1,1]{1,0,3,2:T(4,128)}, u32[]{:S(2)}) copy-start(f32[4,24,1,1]{1,0,3,2:T(4,128)} %constant.98) | copy-start | bytes 1156
  142.1 0.8 copy-start.3
Sparse Core Ops, SparseCore 0:
  64.2 56.0 all-gather.3
